TPU v7x, 128 devices: a whole 4x4x4 slice. The times are simulated.
128 devices in a mesh: row: 8 (over y, core), col: 16 (over x, z).
Axes of the slice: x: 4, y: 4, z: 4, core: 2. Of those that a mesh axis runs over, the one named last changes fastest.
Arguments:
- b_tensor: bfloat16 [128, 1024, 1024], P('col', 'row'), may hold values from -6 to 6
- occ_green: bfloat16 [1024, 1024], P(('row', 'col')), may hold values from -0.1875 to 0.1875
- virt_green: bfloat16 [1024, 1024], P(('row', 'col')), may hold values from -0.1875 to 0.1875
- b_mask: int32 [1, 8, 8], replicated, may hold values 0 or 1
- occ_mask: int32 [8, 8], replicated, may hold values 0 or 1
- virt_mask: int32 [8, 8], replicated, may hold values 0 or 1
Outputs:
- chi: float32 [128, 128], P(('row', 'col'))
All inputs are finite; a program needn't handle non-finite values.
Results may differ from a plain program's by a relative error of at most 0.0041.
Values may be sent and summed in bfloat16 or wider, within the bound.
A program may use at most 64 MiB of HBM per device.

v0:
```python
import jax
import jax.numpy as jnp
from jax import lax
from jax.sharding import PartitionSpec as P

TILE = 128


def expand_pair(mask):
    return jnp.repeat(jnp.repeat(mask, TILE, axis=0), TILE, axis=1).astype(jnp.bfloat16)


def per_device(b_tensor, occ_green, virt_green, b_mask, occ_mask, virt_mask):
    col_index = lax.axis_index("col")
    row_index = lax.axis_index("row")
    p_count, m_count, n_basis = b_tensor.shape
    p_tiles = (col_index * p_count + jnp.arange(p_count, dtype=jnp.int32)) // TILE
    m_tiles = (row_index * m_count + jnp.arange(m_count, dtype=jnp.int32)) // TILE
    local_mask = jnp.take(jnp.take(b_mask, p_tiles, axis=0), m_tiles, axis=1).astype(jnp.bfloat16)
    masked = b_tensor * jnp.repeat(local_mask, TILE, axis=2)
    exchanged_b = lax.all_to_all(masked, "col", split_axis=2, concat_axis=0, tiled=True)
    virt_full = lax.all_gather(virt_green, ("row", "col"), axis=0, tiled=True) * expand_pair(
        virt_mask
    )
    occ_rows = lax.all_gather(occ_green, "col", axis=0, tiled=True)
    occ_rows = occ_rows * lax.dynamic_slice_in_dim(
        expand_pair(occ_mask), row_index * m_count, m_count, 0
    )
    inner = jnp.dot(masked.reshape(-1, n_basis), virt_full, preferred_element_type=jnp.float32)
    inner = inner.astype(jnp.bfloat16).reshape(masked.shape)
    outer = jnp.einsum(
        "lm,pms->pls",
        occ_rows,
        lax.all_gather(inner, "row", axis=1, tiled=True),
        preferred_element_type=jnp.float32,
    ).astype(jnp.bfloat16)
    moved = lax.all_to_all(outer, "col", split_axis=2, concat_axis=0, tiled=True)
    b_flat = exchanged_b.reshape(exchanged_b.shape[0], -1)
    y_flat = moved.reshape(moved.shape[0], -1)
    summed = lax.psum_scatter(
        lax.dot_general(
            y_flat, b_flat, (((1,), (1,)), ((), ())), preferred_element_type=jnp.float32
        ),
        ("row", "col"),
        scatter_dimension=0,
        tiled=True,
    )
    return summed * (-2.0 / n_basis)


def solution(mesh):
    return jax.shard_map(
        per_device,
        mesh=mesh,
        in_specs=(
            P("col", "row", None),
            P(("row", "col"), None),
            P(("row", "col"), None),
            P(),
            P(),
            P(),
        ),
        out_specs=P(("row", "col"), None),
        check_vma=False,
    )
```

profile of v0, /device:TPU:1, one launch (start us, length us, event | category | flops | bytes accessed | tf_op | source)
XLA Modules:
  0.0 387.0 jit_solution(18253904898014795396)
XLA Ops:
  6.5 0.0 all-gather.3.cloned.1.call-start
  6.5 0.7 all-gather.3.cloned.1.call-update
  7.3 0.0 all-gather.5.cloned.1.call-start
  7.4 0.8 broadcast_select_fusion
  8.1 0.8 gather_fusion
  8.9 0.2 fusion.3
  9.2 1.4 broadcast_in_dim.39
  10.5 0.0 copy-start.1
  10.5 2.3 reshape.157
  12.8 0.0 copy-done.1
  12.8 3.2 mul.24
  16.1 63.1 %all-gather.3.cloned.1.call-done = bf16[1024,1024]{1,0:T(8,128)(2,1)} async-done(((bf16[8,1024]{1,0:T(8,128)(2,1)}), bf16[1024,1024]{1,0:T(8,128)(2,1)}) %all-gather.3.cloned.1.call-update) | async-done | bytes 2097168 | tf_op jit(solution)/shard_map/all_gather | solution.py:22
  79.2 0.0 copy-start.3
  79.3 2.9 broadcast_in_dim.41
  82.2 0.0 copy-done.3
  82.2 3.7 fusion.2
  85.9 3.9 %copy.19 = bf16[8,128,1024]{1,2,0:T(8,128)(2,1)} copy(bf16[8,128,1024]{2,1,0:T(8,128)(2,1)} %bitcast.45) | data formatting | bytes 4194304 | tf_op jit(solution)/shard_map/reshape | solution.py:30
  89.8 0.0 all-gather.5.cloned.1.call-update
  89.9 2.9 copy.22
  92.8 0.0 copy-start.2
  92.8 4.2 %all-to-all-start.1 = ((bf16[8,128,1024]{1,0,2:T(8,128)(2,1)}), bf16[8,128,1024]{1,0,2:T(8,128)(2,1)S(1)}, u32[]{:S(2)}, u32[]{:S(2)}) async-start(bf16[8,128,1024]{1,0,2:T(8,128)(2,1)} %copy.22), calls=%async_computation.1 | async-start | bytes 4194304 | tf_op jit(solution)/shard_map/all_to_all | solution.py:21
  97.0 0.0 copy-done.2
  97.1 2.9 broadcast_in_dim.43
  100.0 0.0 copy-start
  100.1 2.0 copy.35
  102.0 0.0 copy-done
  102.0 36.4 %all_gather.11 = bf16[128,1024]{1,0:T(8,128)(2,1)S(1)} all-gather(bf16[8,1024]{1,0:T(8,128)(2,1)S(1)} %copy-done), channel_id=1, replica_groups=mesh['row'=8,'col'=16] {'col'}, dimensions={0}, use_global_device_ids=true | all-gather | bytes 278528 | tf_op jit(solution)/shard_map/all_gather | solution.py:25
  138.5 39.3 %all-gather.5.cloned.1.call-done = bf16[8,1024,1024]{1,2,0:T(8,128)(2,1)} async-done(((bf16[8,128,1024]{1,2,0:T(8,128)(2,1)}), bf16[8,1024,1024]{1,2,0:T(8,128)(2,1)}) %all-gather.5.cloned.1.call-update) | async-done | bytes 16777232 | tf_op jit(solution)/shard_map/all_gather | solution.py:34
  177.7 10.3 %convert_bitcast_fusion = bf16[8,128,1024]{1,2,0:T(8,128)(2,1)S(1)} fusion(bf16[8,1024,1024]{1,2,0:T(8,128)(2,1)} %all-gather.5.cloned.1.call-done, bf16[128,1024]{1,0:T(8,128)(2,1)S(1)} %all_gather.11, bf16[1024,1024]{1,0:T(8,128)(2,1)} %bitcast.44, s32[]{:T(128)S(6)} %select_n.83), kind=kOutput, calls=%fused_computation.5 | convolution fusion | flops 2149056512 | bytes 19398660 | tf_op jit(solution)/shard_map/lm,pms->pls/dot_general | solution.py:31
  188.0 2.7 copy.20
  190.7 0.0 all-to-all-done.1
  190.7 6.7 %all-to-all-start = ((bf16[8,128,1024]{1,0,2:T(8,128)(2,1)}), bf16[8,128,1024]{1,0,2:T(8,128)(2,1)}, u32[]{:S(2)}, u32[]{:S(2)}) async-start(bf16[8,128,1024]{1,0,2:T(8,128)(2,1)} %copy.20), calls=%async_computation | async-start | bytes 4194304 | tf_op jit(solution)/shard_map/all_to_all | solution.py:37
  197.5 0.0 all-reduce.3.cloned.1.call-start
  197.5 3.2 copy.24
  200.7 5.7 %reshape.161 = bf16[128,8192]{1,0:T(8,128)(2,1)S(1)} reshape(bf16[16,8,128,64]{3,2,1,0:T(8,128)(2,1)} %copy.24) | data formatting | bytes 4194304 | tf_op jit(solution)/shard_map/reshape | solution.py:38
  206.4 20.3 %all-to-all-done = bf16[8,128,1024]{1,0,2:T(8,128)(2,1)} async-done(((bf16[8,128,1024]{1,0,2:T(8,128)(2,1)}), bf16[8,128,1024]{1,0,2:T(8,128)(2,1)}, u32[]{:S(2)}, u32[]{:S(2)}) %all-to-all-start) | async-done | bytes 2097184 | tf_op jit(solution)/shard_map/all_to_all | solution.py:37
  226.7 4.8 %copy.21 = bf16[8,128,16,64]{3,1,0,2:T(8,128)(2,1)} copy(bf16[8,128,16,64]{1,0,3,2:T(8,128)(2,1)} %bitcast.9) | data formatting | bytes 4194304 | tf_op jit(solution)/shard_map/all_to_all | solution.py:37
  231.5 6.6 %reshape.160 = bf16[128,8192]{1,0:T(8,128)(2,1)} reshape(bf16[16,8,128,64]{3,2,1,0:T(8,128)(2,1)} %bitcast.39) | data formatting | bytes 4194304 | tf_op jit(solution)/shard_map/reshape | solution.py:39
  238.1 2.9 fusion.9
  241.1 0.0 all-reduce.3.cloned.1.call-update
  241.1 138.1 %all-reduce.3.cloned.1.call-done = f32[128,128]{1,0:T(8,128)} async-done(((f32[128,128]{1,0:T(8,128)}), f32[128,128]{1,0:T(8,128)}) %all-reduce.3.cloned.1.call-update) | async-done | bytes 65552
  379.2 1.2 dynamic-slice_multiply_fusion
  (9 shorter events, 0.2 us)
Async XLA Ops:
  6.5 72.7 %all-gather.3.cloned.1.call-start = ((), (), s32[]{:S(2)}) async-start(), calls=%async_computation.2 | async-start | bytes 2113536 | tf_op jit(solution)/shard_map/all_gather | solution.py:22
  7.3 170.5 %all-gather.5.cloned.1.call-start = ((), (), s32[]{:S(2)}) async-start(), calls=%async_computation.3 | async-start | bytes 18874368 | tf_op jit(solution)/shard_map/all_gather | solution.py:34
  10.5 2.3 copy-start.1
  79.2 3.0 copy-start.3
  92.8 4.2 %copy-start.2 = (s32[8,8]{1,0:T(8,128)S(1)}, s32[8,8]{1,0:T(8,128)}, u32[]{:S(2)}) copy-start(s32[8,8]{1,0:T(8,128)} %param.10) | copy-start | bytes 772
  92.8 97.9 %all-to-all-start.1 = ((bf16[8,128,1024]{1,0,2:T(8,128)(2,1)}), bf16[8,128,1024]{1,0,2:T(8,128)(2,1)S(1)}, u32[]{:S(2)}, u32[]{:S(2)}) async-start(bf16[8,128,1024]{1,0,2:T(8,128)(2,1)} %copy.22), calls=%async_computation.1 | async-start | bytes 4194304 | tf_op jit(solution)/shard_map/all_to_all | solution.py:21
  100.0 2.0 copy-start
  190.7 36.0 %all-to-all-start = ((bf16[8,128,1024]{1,0,2:T(8,128)(2,1)}), bf16[8,128,1024]{1,0,2:T(8,128)(2,1)}, u32[]{:S(2)}, u32[]{:S(2)}) async-start(bf16[8,128,1024]{1,0,2:T(8,128)(2,1)} %copy.20), calls=%async_computation | async-start | bytes 4194304 | tf_op jit(solution)/shard_map/all_to_all | solution.py:37
  197.5 181.8 %all-reduce.3.cloned.1.call-start = ((), (), s32[]{:S(2)}) async-start(), calls=%async_computation.4 | async-start | bytes 131072
Sparse Core Ops, SparseCore 0:
  10.3 68.8 all-gather.2
  90.0 87.6 all-gather.4
  241.2 137.9 all-reduce.2
where the time goes:
time: 388 us; the launch traced here: 387 us
  waiting for transfers between devices  262 us (68%)
  local copies, waits for them, and re-layouts  42.2 us (11%)
  blocking collectives  36.4 us (9%)
  matrix products  16.9 us (4%)
  between operations  13.3 us (3%)
  starting transfers between devices  11 us (3%)
  other arithmetic  5.47 us (1%)
    unnamed x4, waiting for transfers between devices  139 us
    all_gather x1, waiting for transfers between devices, per_device(): lax.all_gather(virt_green, ('row', 'col'), axis=0, tiled=True)  63.1 us
    all_gather x1, waiting for transfers between devices, per_device(): lax.all_gather(inner, 'row', axis=1, tiled=True)  39.3 us
    all_gather x1, blocking collectives, per_device(): occ_rows = lax.all_gather(occ_green, 'col', axis=0, tiled=True)  36.4 us
    all_to_all x1, waiting for transfers between devices, per_device(): lax.all_to_all(outer, 'col', split_axis=2, concat_axis=0, tiled=True)  20.3 us
    dot_general x1, matrix products, per_device(): jnp.einsum('lm,pms->pls', occ_rows, lax.all_gather(inner, 'row', axis=1,...  10.3 us
  transfers between devices with their start and end apart: 5, of which 4 were waited for; matrix products, arithmetic and copies ran while one was open for 10% of the time, Pallas kernels for 0%

commit v1 on v0

--- a/solution.py
+++ b/solution.py
@@ -11,6 +11,19 @@
 
 
 def per_device(b_tensor, occ_green, virt_green, b_mask, occ_mask, virt_mask):
+
+    def map_tracks_over_axis(xs):
+        heard = jnp.concatenate(
+            lax.all_to_all(
+                jnp.stack([xs for _ in range(lax.psum(1, axis_name="col"))], 0),
+                axis_name="col",
+                split_axis=0,
+                concat_axis=0,
+            ),
+            0,
+        )
+        return heard
+
     col_index = lax.axis_index("col")
     row_index = lax.axis_index("row")
     p_count, m_count, n_basis = b_tensor.shape
@@ -22,7 +35,7 @@
     virt_full = lax.all_gather(virt_green, ("row", "col"), axis=0, tiled=True) * expand_pair(
         virt_mask
     )
-    occ_rows = lax.all_gather(occ_green, "col", axis=0, tiled=True)
+    occ_rows = map_tracks_over_axis(occ_green)
     occ_rows = occ_rows * lax.dynamic_slice_in_dim(
         expand_pair(occ_mask), row_index * m_count, m_count, 0
     )

time: 388 us -> 388 us (level)
  blocking collectives: 36.4 us -> 0 us
  waiting for transfers between devices: 262 us -> 293 us
    all_gather x1 -> x0, blocking collectives: 36.4 us -> none  [per_device(): occ_rows = lax.all_gather(occ_green, 'col', axis=0, tiled=True)]
    all_gather x1, waiting for transfers between devices: 39.3 us -> 65.7 us  [per_device(): lax.all_gather(inner, 'row', axis=1, tiled=True)]
    all_to_all x0 -> x1, waiting for transfers between devices: none -> 4.78 us  [map_tracks_over_axis(): lax.all_to_all(jnp.stack([xs for _ in range(lax.psum(1, axis_name='col'))...]
    all_to_all x0 -> x1, starting transfers between devices: none -> 4.09 us  [map_tracks_over_axis(): lax.all_to_all(jnp.stack([xs for _ in range(lax.psum(1, axis_name='col'))...]
  transfers between devices with their start and end apart: 5 -> 6, of which waited for: 4 -> 5; matrix products, arithmetic and copies ran while one was open for 10% -> 10% of each run, Pallas kernels for 0% -> 0%
where the time goes in v1:
time: 388 us; the launch traced here: 387 us
  waiting for transfers between devices  293 us (76%)
  local copies, waits for them, and re-layouts  43.8 us (11%)
  matrix products  16.9 us (4%)
  starting transfers between devices  14.8 us (4%)
  between operations  13.3 us (3%)
  other arithmetic  5.46 us (1%)
    unnamed x4, waiting for transfers between devices  139 us
    all_gather x1, waiting for transfers between devices, per_device(): lax.all_gather(inner, 'row', axis=1, tiled=True)  65.7 us
    all_gather x1, waiting for transfers between devices, per_device(): lax.all_gather(virt_green, ('row', 'col'), axis=0, tiled=True)  63.1 us
    all_to_all x1, waiting for transfers between devices, per_device(): lax.all_to_all(outer, 'col', split_axis=2, concat_axis=0, tiled=True)  20.3 us
    dot_general x1, matrix products, per_device(): jnp.einsum('lm,pms->pls', occ_rows, lax.all_gather(inner, 'row', axis=1,...  10.3 us
  transfers between devices with their start and end apart: 6, of which 5 were waited for; matrix products, arithmetic and copies ran while one was open for 10% of the time, Pallas kernels for 0%

profile of v1, /device:TPU:1, one launch (start us, length us, event | category | flops | bytes accessed | tf_op | source)
XLA Modules:
  0.0 387.0 jit_solution(13422273665811436567)
XLA Ops:
  6.5 0.0 all-gather.3.cloned.1.call-start
  6.5 0.7 all-gather.3.cloned.1.call-update
  7.3 0.0 all-gather.5.cloned.1.call-start
  7.4 0.8 broadcast_select_fusion
  8.1 0.8 gather_fusion
  8.9 0.2 fusion.3
  9.2 1.4 broadcast_in_dim.39
  10.5 0.0 copy-start.1
  10.5 2.3 reshape.162
  12.9 0.0 copy-done.1
  12.9 3.2 mul.24
  16.1 63.1 %all-gather.3.cloned.1.call-done = bf16[1024,1024]{1,0:T(8,128)(2,1)} async-done(((bf16[8,1024]{1,0:T(8,128)(2,1)}), bf16[1024,1024]{1,0:T(8,128)(2,1)}) %all-gather.3.cloned.1.call-update) | async-done | bytes 2097168 | tf_op jit(solution)/shard_map/all_gather | solution.py:35
  79.2 0.0 copy-start.3
  79.3 2.9 broadcast_in_dim.41
  82.2 0.0 copy-done.3
  82.2 3.7 fusion.2
  85.9 3.9 %copy.19 = bf16[8,128,1024]{1,2,0:T(8,128)(2,1)} copy(bf16[8,128,1024]{2,1,0:T(8,128)(2,1)} %bitcast.50) | data formatting | bytes 4194304 | tf_op jit(solution)/shard_map/reshape | solution.py:43
  89.9 0.0 copy-start
  89.9 0.0 all-gather.5.cloned.1.call-update
  89.9 0.7 copy-done
  90.6 0.7 stack.2
  91.3 4.1 %all-to-all-start = ((bf16[16,8,1024]{2,1,0:T(8,128)(2,1)}), bf16[16,8,1024]{2,1,0:T(8,128)(2,1)S(1)}, u32[]{:S(2)}, u32[]{:S(2)}) async-start(bf16[16,8,1024]{2,1,0:T(8,128)(2,1)} %stack.2), calls=%async_computation | async-start | bytes 524288 | tf_op jit(solution)/shard_map/all_to_all | solution.py:17
  95.4 2.9 copy.22
  98.3 0.0 copy-start.2
  98.3 4.8 %all-to-all-done = bf16[16,8,1024]{2,1,0:T(8,128)(2,1)S(1)} async-done(((bf16[16,8,1024]{2,1,0:T(8,128)(2,1)}), bf16[16,8,1024]{2,1,0:T(8,128)(2,1)S(1)}, u32[]{:S(2)}, u32[]{:S(2)}) %all-to-all-start) | async-done | bytes 262176 | tf_op jit(solution)/shard_map/all_to_all | solution.py:17
  103.1 3.9 %all-to-all-start.2 = ((bf16[8,128,1024]{1,0,2:T(8,128)(2,1)}), bf16[8,128,1024]{1,0,2:T(8,128)(2,1)S(1)}, u32[]{:S(2)}, u32[]{:S(2)}) async-start(bf16[8,128,1024]{1,0,2:T(8,128)(2,1)} %copy.22), calls=%async_computation.2 | async-start | bytes 4194304 | tf_op jit(solution)/shard_map/all_to_all | solution.py:34
  107.0 0.0 copy-done.2
  107.1 2.9 broadcast_in_dim.43
  110.1 2.0 copy.35
  112.0 65.7 %all-gather.5.cloned.1.call-done = bf16[8,1024,1024]{1,2,0:T(8,128)(2,1)} async-done(((bf16[8,128,1024]{1,2,0:T(8,128)(2,1)}), bf16[8,1024,1024]{1,2,0:T(8,128)(2,1)}) %all-gather.5.cloned.1.call-update) | async-done | bytes 16777232 | tf_op jit(solution)/shard_map/all_gather | solution.py:47
  177.7 10.3 %convert_bitcast_fusion = bf16[8,128,1024]{1,2,0:T(8,128)(2,1)S(1)} fusion(bf16[8,1024,1024]{1,2,0:T(8,128)(2,1)} %all-gather.5.cloned.1.call-done, bf16[16,8,1024]{2,1,0:T(8,128)(2,1)S(1)} %all-to-all-done, bf16[1024,1024]{1,0:T(8,128)(2,1)} %bitcast.49, s32[]{:T(128)S(6)} %select_n.83), kind=kOutput, calls=%fused_computation.5 | convolution fusion | flops 2149056512 | bytes 19398660 | tf_op jit(solution)/shard_map/lm,pms->pls/dot_general | solution.py:44
  188.1 2.7 copy.20
  190.8 0.0 all-to-all-done.2
  190.8 6.7 %all-to-all-start.1 = ((bf16[8,128,1024]{1,0,2:T(8,128)(2,1)}), bf16[8,128,1024]{1,0,2:T(8,128)(2,1)}, u32[]{:S(2)}, u32[]{:S(2)}) async-start(bf16[8,128,1024]{1,0,2:T(8,128)(2,1)} %copy.20), calls=%async_computation.1 | async-start | bytes 4194304 | tf_op jit(solution)/shard_map/all_to_all | solution.py:50
  197.5 0.0 all-reduce.3.cloned.1.call-start
  197.5 3.2 copy.24
  200.8 5.7 %reshape.167 = bf16[128,8192]{1,0:T(8,128)(2,1)S(1)} reshape(bf16[16,8,128,64]{3,2,1,0:T(8,128)(2,1)} %copy.24) | data formatting | bytes 4194304 | tf_op jit(solution)/shard_map/reshape | solution.py:51
  206.4 20.3 %all-to-all-done.1 = bf16[8,128,1024]{1,0,2:T(8,128)(2,1)} async-done(((bf16[8,128,1024]{1,0,2:T(8,128)(2,1)}), bf16[8,128,1024]{1,0,2:T(8,128)(2,1)}, u32[]{:S(2)}, u32[]{:S(2)}) %all-to-all-start.1) | async-done | bytes 2097184 | tf_op jit(solution)/shard_map/all_to_all | solution.py:50
  226.7 4.8 %copy.21 = bf16[8,128,16,64]{3,1,0,2:T(8,128)(2,1)} copy(bf16[8,128,16,64]{1,0,3,2:T(8,128)(2,1)} %bitcast.10) | data formatting | bytes 4194304 | tf_op jit(solution)/shard_map/all_to_all | solution.py:50
  231.6 6.6 %reshape.166 = bf16[128,8192]{1,0:T(8,128)(2,1)} reshape(bf16[16,8,128,64]{3,2,1,0:T(8,128)(2,1)} %bitcast.44) | data formatting | bytes 4194304 | tf_op jit(solution)/shard_map/reshape | solution.py:52
  238.2 2.9 fusion.8
  241.1 0.0 all-reduce.3.cloned.1.call-update
  241.1 138.2 %all-reduce.3.cloned.1.call-done = f32[128,128]{1,0:T(8,128)} async-done(((f32[128,128]{1,0:T(8,128)}), f32[128,128]{1,0:T(8,128)}) %all-reduce.3.cloned.1.call-update) | async-done | bytes 65552
  379.3 1.2 dynamic-slice_multiply_fusion
  (9 shorter events, 0.2 us)
Async XLA Ops:
  6.5 72.7 %all-gather.3.cloned.1.call-start = ((), (), s32[]{:S(2)}) async-start(), calls=%async_computation.3 | async-start | bytes 2113536 | tf_op jit(solution)/shard_map/all_gather | solution.py:35
  7.3 170.5 %all-gather.5.cloned.1.call-start = ((), (), s32[]{:S(2)}) async-start(), calls=%async_computation.4 | async-start | bytes 18874368 | tf_op jit(solution)/shard_map/all_gather | solution.py:47
  10.5 2.3 copy-start.1
  79.2 3.0 copy-start.3
  89.9 0.7 copy-start
  91.3 11.8 %all-to-all-start = ((bf16[16,8,1024]{2,1,0:T(8,128)(2,1)}), bf16[16,8,1024]{2,1,0:T(8,128)(2,1)S(1)}, u32[]{:S(2)}, u32[]{:S(2)}) async-start(bf16[16,8,1024]{2,1,0:T(8,128)(2,1)} %stack.2), calls=%async_computation | async-start | bytes 524288 | tf_op jit(solution)/shard_map/all_to_all | solution.py:17
  98.3 8.7 %copy-start.2 = (s32[8,8]{1,0:T(8,128)S(1)}, s32[8,8]{1,0:T(8,128)}, u32[]{:S(2)}) copy-start(s32[8,8]{1,0:T(8,128)} %param.10) | copy-start | bytes 772
  103.1 87.6 %all-to-all-start.2 = ((bf16[8,128,1024]{1,0,2:T(8,128)(2,1)}), bf16[8,128,1024]{1,0,2:T(8,128)(2,1)S(1)}, u32[]{:S(2)}, u32[]{:S(2)}) async-start(bf16[8,128,1024]{1,0,2:T(8,128)(2,1)} %copy.22), calls=%async_computation.2 | async-start | bytes 4194304 | tf_op jit(solution)/shard_map/all_to_all | solution.py:34
  190.8 36.0 %all-to-all-start.1 = ((bf16[8,128,1024]{1,0,2:T(8,128)(2,1)}), bf16[8,128,1024]{1,0,2:T(8,128)(2,1)}, u32[]{:S(2)}, u32[]{:S(2)}) async-start(bf16[8,128,1024]{1,0,2:T(8,128)(2,1)} %copy.20), calls=%async_computation.1 | async-start | bytes 4194304 | tf_op jit(solution)/shard_map/all_to_all | solution.py:50
  197.5 181.8 %all-reduce.3.cloned.1.call-start = ((), (), s32[]{:S(2)}) async-start(), calls=%async_computation.5 | async-start | bytes 131072
Sparse Core Ops, SparseCore 0:
  10.3 68.8 all-gather.2
  90.0 87.6 all-gather.4
  241.3 138.0 all-reduce.2
